TPU v7x, 32 devices: a whole 2x2x4 slice. The times are simulated.
32 devices in a mesh: grp: 1, rows: 32 (over z, y, x, core).
Axes of the slice: x: 2, y: 2, z: 4, core: 2. Of those that a mesh axis runs over, the one named last changes fastest.
Arguments:
- embeddings: bfloat16 [16384, 1024], P(('grp', 'rows')), may hold values from -30 to 30
- centroids: bfloat16 [4096, 1024], replicated, may hold values from -0.1875 to 0.1875
- log_weights: float32 [4096], replicated, may hold values from -1 to 1
Outputs:
- new_centroids: bfloat16 [4096, 1024], P(('grp', 'rows'))
- new_log_weights: float32 [4096], P(('grp', 'rows'))
- log_normalizer: float32 [16384], P(('grp', 'rows'))
All inputs are finite; a program needn't handle non-finite values.
Results may differ from a plain program's by a relative error of at most 0.0034.
Values may be sent and summed in bfloat16 or wider, within the bound.
A program may use at most 128 MiB of HBM per device.

v0:
```python
import jax
import jax.numpy as jnp
from jax import lax
from jax.sharding import PartitionSpec as P

KAPPA = 32


def local(embeddings, centroids, log_weights):
    embed_float = embeddings.astype(jnp.float32)
    unit_rows = (
        embed_float * lax.rsqrt(jnp.sum(embed_float * embed_float, 1, keepdims=True) + 1e-06)
    ).astype(jnp.bfloat16)
    scores = (
        KAPPA * jnp.dot(unit_rows, centroids.T, preferred_element_type=jnp.float32) + log_weights
    )
    exponent = jnp.exp(scores)
    responsible = (exponent / jnp.sum(exponent, 1, keepdims=True)).astype(jnp.bfloat16)
    counts = lax.psum(jnp.sum(responsible.astype(jnp.float32), 0), "rows")
    row_total = unit_rows.shape[0] * lax.axis_size("rows")
    new_log_weights = jnp.log(counts / row_total)
    term_sums = jnp.dot(responsible.T, unit_rows, preferred_element_type=jnp.float32)
    comp_dev = centroids.shape[0] // lax.axis_size("rows")
    own_start = lax.axis_index("rows") * comp_dev
    own_log_weights = lax.dynamic_slice_in_dim(new_log_weights, own_start, comp_dev)
    own_sums = lax.psum_scatter(term_sums, "rows", scatter_dimension=0, tiled=True)
    directions = (
        own_sums * lax.rsqrt(jnp.sum(own_sums * own_sums, 1, keepdims=True) + 1e-06)
    ).astype(jnp.bfloat16)
    block_scores = (
        KAPPA
        * jnp.dot(
            unit_rows,
            lax.all_gather(directions, "rows", axis=0, tiled=True).T,
            preferred_element_type=jnp.float32,
        )
        + new_log_weights
    )
    exp_total = jnp.sum(jnp.exp(block_scores), 1)
    return (directions, own_log_weights, jnp.log(exp_total))


def solution(mesh):
    return jax.shard_map(
        local,
        mesh=mesh,
        in_specs=(P(("grp", "rows"), None), P(), P()),
        out_specs=(P(("grp", "rows"), None), P(("grp", "rows")), P(("grp", "rows"))),
        check_vma=False,
    )
```

profile of v0, /device:TPU:0, one launch (start us, length us, event | category | flops | bytes accessed | tf_op | source)
XLA Modules:
  0.0 312.6 jit_solution(6081287427242209415)
XLA Ops:
  7.2 0.0 reduce-scatter.2.cloned.1.call-start
  7.2 1.5 fusion.1
  8.7 0.0 copy-start.1
  8.7 8.8 %fusion = (f32[512]{0:T(512)S(1)}, f32[512,4096]{1,0:T(8,128)S(1)}) fusion(f32[4096]{0:T(1024)} %param.5, bf16[4096,1024]{1,0:T(8,128)(2,1)} %param.4, bf16[512,1024]{1,0:T(8,128)(2,1)} %param.3, f32[512]{0:T(512)S(1)} %add_rsqrt_fusion), kind=kOutput, calls=%fused_computation.4 | convolution fusion | flops 4302831104 | bytes 17846272 | tf_op jit(solution)/shard_map/dot_general | solution.py:15
  17.5 0.0 copy-start
  17.5 0.0 copy-done.1
  17.5 2.1 convert_reduce_fusion
  19.6 0.0 copy-done
  19.7 8.3 %fusion.4 = f32[4096,1024]{1,0:T(8,128)} fusion(bf16[512,4096]{1,0:T(8,128)(2,1)S(1)} %get-tuple-element.4, bf16[512,1024]{1,0:T(8,128)(2,1)S(1)} %copy-done, f32[512]{0:T(512)S(1)} %add_rsqrt_fusion), kind=kOutput, calls=%fused_computation.14 | convolution fusion | flops 4296540160 | bytes 22022144 | tf_op jit(solution)/shard_map/dot_general | solution.py:22
  28.0 0.0 reduce-scatter.2.cloned.1.call-update
  28.0 0.0 all-gather.2.cloned.1.call-start
  28.1 185.7 %reduce-scatter.2.cloned.1.call-done = f32[128,1024]{1,0:T(8,128)} async-done(((f32[4096,1024]{1,0:T(8,128)}), f32[128,1024]{1,0:T(8,128)}) %reduce-scatter.2.cloned.1.call-update) | async-done | bytes 524304 | tf_op jit(solution)/shard_map/reduce_scatter | solution.py:26
  213.8 1.2 multiply_reduce_fusion
  215.0 1.8 multiply_convert_fusion
  216.8 0.0 all-gather.2.cloned.1.call-update
  216.8 43.1 %psum.7 = f32[4096]{0:T(1024)S(1)} all-reduce(f32[4096]{0:T(1024)S(1)} %get-tuple-element.3), channel_id=1, replica_groups=mesh['grp'=1,'rows'=32] {'rows'}, use_global_device_ids=true, to_apply=%region_5.0 | all-reduce | flops 4096 | bytes 32768 | tf_op jit(solution)/shard_map/psum | solution.py:19
  259.9 0.6 dynamic_slice.3
  260.5 35.6 %all-gather.2.cloned.1.call-done = bf16[4096,1024]{1,0:T(8,128)(2,1)} async-done(((bf16[128,1024]{1,0:T(8,128)(2,1)}), bf16[4096,1024]{1,0:T(8,128)(2,1)}) %all-gather.2.cloned.1.call-update) | async-done | bytes 8388624 | tf_op jit(solution)/shard_map/all_gather | solution.py:34
  296.1 9.0 %exponential_reduce_fusion = f32[512]{0:T(512)S(1)} fusion(bf16[4096,1024]{1,0:T(8,128)(2,1)} %all-gather.2.cloned.1.call-done, f32[4096]{0:T(1024)S(1)} %multiply_log_fusion, bf16[512,1024]{1,0:T(8,128)(2,1)S(1)} %copy-done, f32[512]{0:T(512)S(1)} %add_rsqrt_fusion), kind=kOutput, calls=%fused_computation | convolution fusion | flops 4302831104 | bytes 9457664 | tf_op jit(solution)/shard_map/dot_general | solution.py:32
  305.2 0.6 log.7
  (3 shorter events, 0.0 us)
Async XLA Ops:
  7.2 206.6 %reduce-scatter.2.cloned.1.call-start = ((), (), s32[]{:S(2)}) async-start(), calls=%async_computation.1 | async-start | bytes 17301504 | tf_op jit(solution)/shard_map/reduce_scatter | solution.py:26
  8.7 8.8 %copy-start.1 = (f32[4096]{0:T(1024)S(1)}, f32[4096]{0:T(1024)}, u32[]{:S(2)}) copy-start(f32[4096]{0:T(1024)} %param.5) | copy-start | bytes 49156
  17.5 2.1 copy-start
  28.0 268.1 %all-gather.2.cloned.1.call-start = ((), (), s32[]{:S(2)}) async-start(), calls=%async_computation.2 | async-start | bytes 8650752 | tf_op jit(solution)/shard_map/all_gather | solution.py:34
Sparse Core Ops, SparseCore 0:
  28.1 185.6 reduce-scatter.1
  217.2 78.8 all-gather.1
where the time goes:
time: 313 us
  waiting for transfers between devices  221 us (71%)
  blocking collectives  43.1 us (14%)
  matrix products  26.1 us (8%)
  between operations  14.1 us (5%)
  other arithmetic  6.64 us (2%)
    reduce_scatter x1, waiting for transfers between devices, local(): lax.psum_scatter(term_sums, 'rows', scatter_dimension=0, tiled=True)  186 us
    psum x1, blocking collectives, local(): counts = lax.psum(jnp.sum(responsible.astype(jnp.float32), 0), 'rows')  43.1 us
    all_gather x1, waiting for transfers between devices, local(): lax.all_gather(directions, 'rows', axis=0, tiled=True)  35.6 us
    dot_general x1, matrix products, local(): jnp.dot(unit_rows, lax.all_gather(directions, 'rows', axis=0, tiled=True)...  9.04 us
    dot_general x1, matrix products, local(): jnp.dot(unit_rows, centroids.T, preferred_element_type=jnp.float32)  8.77 us
    dot_general x1, matrix products, local(): jnp.dot(responsible.T, unit_rows, preferred_element_type=jnp.float32)  8.32 us
  transfers between devices with their start and end apart: 2, of which 2 were waited for; matrix products, arithmetic and copies ran while one was open for 0% of the time, Pallas kernels for 0%

commit v1 on v0

v1 whole, which is shorter than its diff:
```python
import functools

import jax
import jax.numpy as jnp
from jax import lax
from jax.experimental import pallas as pl
from jax.experimental.pallas import tpu as pltpu
from jax.sharding import PartitionSpec as P

KAPPA = 32
GROUP = 8
MESH = pl.DeviceIdType.MESH
NT = (((1,), (1,)), ((), ()))


def kernel(
    zs, nrows, dchunk, emb_ref, cent_hbm, lw_ref, dir_ref, nlw_ref, lse_ref,
    unit, cent, expo, resp, rsum, rsum_all, send_buf, recv_buf, cnt_send, cnt_recv,
    own_sum, gathered, nlw_all, part, part_recv,
    cent_sem, row_ssem, row_rsem, rs_ssem, rs_rsem, sc_ssem, sc_rsem,
    cn_ssem, cn_rsem, ag_ssem, ag_rsem, nl_ssem, nl_rsem, fin_ssem, fin_rsem,
):
    rows, depth = emb_ref.shape
    half = rows // 2
    comp = dir_ref.shape[0]
    chunks = depth // dchunk
    comps = zs * comp
    me = lax.axis_index("rows")
    z = me // GROUP
    p = me % GROUP

    def plane(mask):
        q = p
        for bit in (1, 2, 4):
            if mask & bit:
                q = q + bit - 2 * bit * ((p // bit) % 2)
        return q

    def dev(zz, q):
        return {"rows": zz * GROUP + q}

    def remote(src, dst, ssem, rsem, to):
        return pltpu.make_async_remote_copy(
            src_ref=src, dst_ref=dst, send_sem=ssem, recv_sem=rsem,
            device_id=to, device_id_type=MESH,
        )

    barrier = pltpu.get_barrier_semaphore()
    for mask in range(1, GROUP):
        pl.semaphore_signal(barrier, inc=1, device_id=dev(z, plane(mask)), device_id_type=MESH)
    for o in range(1, zs):
        pl.semaphore_signal(barrier, inc=1, device_id=dev((z + o) % zs, p), device_id_type=MESH)

    cent_copies = [
        pltpu.make_async_copy(
            cent_hbm.at[pl.ds((b * GROUP + p) * comp, comp)],
            cent.at[pl.ds(b * comp, comp)],
            cent_sem.at[b],
        )
        for b in range(zs)
    ]
    for c in cent_copies:
        c.start()

    embed = emb_ref[...].astype(jnp.float32)
    unit[pl.ds(p * rows, rows), :] = (
        embed * lax.rsqrt(jnp.sum(embed * embed, 1, keepdims=True) + 1e-06)
    ).astype(jnp.bfloat16)
    pl.semaphore_wait(barrier, GROUP - 1 + zs - 1)

    def row_copy(dst, blk, h):
        where = unit.at[pl.ds(plane(blk) * rows + h * half, half)]
        m = blk ^ dst
        return remote(
            where, where, row_ssem.at[m, h], row_rsem.at[m, h], dev(z, plane(dst))
        )

    def arrived(m, h):
        where = unit.at[pl.ds(plane(m) * rows + h * half, half)]
        remote(where, where, row_ssem.at[m, h], row_rsem.at[m, h], dev(z, plane(1))).wait_recv()

    sends = []

    def send(dst, blk, h):
        c = row_copy(dst, blk, h)
        c.start()
        sends.append(c)

    send(2, 0, 0)
    send(4, 0, 1)
    send(1, 0, 0)
    send(2, 0, 1)
    send(4, 0, 0)
    send(1, 0, 1)
    for c in cent_copies:
        c.wait()

    def score(m, h):
        base = plane(m) * rows + h * half
        at = pl.ds(pl.multiple_of(base, half), half)
        dots = lax.dot_general(cent[...], unit[at, :], NT, preferred_element_type=jnp.float32)
        e = jnp.exp(KAPPA * dots + lw_ref[...])
        expo[:, at] = e
        rsum[:, at] = jnp.broadcast_to(jnp.sum(e, 0, keepdims=True), (8, half))

    score(0, 0)
    score(0, 1)
    arrived(2, 0)
    send(4, 2, 0)
    send(1, 2, 0)
    arrived(4, 1)
    send(2, 4, 1)
    send(1, 4, 1)
    for h in (0, 1):
        arrived(1, h)
        score(1, h)
    score(2, 0)
    score(4, 1)
    arrived(2, 1)
    send(1, 2, 1)
    arrived(4, 0)
    send(1, 4, 0)
    score(2, 1)
    score(4, 0)
    for m, h in ((3, 0), (5, 1), (3, 1), (5, 0)):
        arrived(m, h)
        score(m, h)
    for h in (0, 1):
        arrived(6, h)
        send(1, 6, h)
    for h in (0, 1):
        score(6, h)
    for h in (0, 1):
        arrived(7, h)
        score(7, h)

    sum_copies = []
    for m in range(1, GROUP):
        c = remote(rsum, rsum_all.at[m], sc_ssem.at[m], sc_rsem.at[m], dev(z, plane(m)))
        c.start()
        sum_copies.append(c)
    for c in sum_copies:
        c.wait_recv()
    total = rsum[...]
    for m in range(1, GROUP):
        total = total + rsum_all[m]
    rsum_all[0] = 1.0 / total

    def normalise(i, carry):
        at = pl.ds(pl.multiple_of(i * half, half), half)
        inv = rsum_all[0, :, at][:1]
        resp[:, at] = (expo[:, at] * inv).astype(jnp.bfloat16)
        return carry

    lax.fori_loop(0, 2 * GROUP, normalise, 0)

    cnt_copies = []
    ones = jnp.ones((8, GROUP * rows), jnp.bfloat16)
    for b in range(zs):
        cnt_send[b, :, :comp] = lax.dot_general(
            ones, resp[pl.ds(b * comp, comp), :], NT, preferred_element_type=jnp.float32
        )
    for o in range(1, zs):
        to = (z + zs - o) % zs
        c = remote(cnt_send.at[to], cnt_recv.at[o], cn_ssem.at[o], cn_rsem.at[o], dev(to, p))
        c.start()
        cnt_copies.append(c)

    rs_copies = []
    for d in range(chunks):
        cols = pl.ds(d * dchunk, dchunk)
        acc = jnp.dot(resp[...], unit[:, cols], preferred_element_type=jnp.float32)
        expo[:, cols] = acc
        send_buf[d] = acc.astype(jnp.bfloat16).reshape(zs, comp, dchunk)
        for o in range(1, zs):
            to = (z + zs - o) % zs
            c = remote(
                send_buf.at[d, to], recv_buf.at[d, o], rs_ssem.at[d, o], rs_rsem.at[d, o],
                dev(to, p),
            )
            c.start()
            rs_copies.append(c)
        own_sum[:, cols] = expo[pl.ds(pl.multiple_of(z * comp, comp), comp), cols]

    for c in cnt_copies:
        c.wait_recv()
    count = cnt_send[z]
    for o in range(1, zs):
        count = count + cnt_recv[o]
    nlw = jnp.log(count[:, :comp] / nrows)
    nlw_all[z, :, :comp] = nlw
    nlw_ref[...] = nlw[:1]

    square = jnp.zeros((comp, 1), jnp.float32)
    for d in range(chunks):
        cols = pl.ds(d * dchunk, dchunk)
        got = own_sum[:, cols]
        for o in range(1, zs):
            rs_copies[d * (zs - 1) + o - 1].wait_recv()
            got = got + recv_buf[d, o].astype(jnp.float32)
        own_sum[:, cols] = got
        square = square + jnp.sum(got * got, 1, keepdims=True)
    direction = (own_sum[...] * lax.rsqrt(square + 1e-06)).astype(jnp.bfloat16)
    gathered[z] = direction
    dir_ref[...] = direction

    ag_copies = []
    for o in range(1, zs):
        to = dev((z + zs - o) % zs, p)
        c = remote(nlw_all.at[z], nlw_all.at[z], nl_ssem.at[o], nl_rsem.at[o], to)
        c.start()
        ag_copies.append(c)
        c = remote(gathered.at[z], gathered.at[z], ag_ssem.at[o], ag_rsem.at[o], to)
        c.start()
        ag_copies.append(c)

    part[...] = jnp.zeros_like(part)
    for o in range(zs):
        b = (z + o) % zs
        if o:
            remote(
                nlw_all.at[b], nlw_all.at[b], nl_ssem.at[o], nl_rsem.at[o], dev(b, p)
            ).wait_recv()
            remote(
                gathered.at[b], gathered.at[b], ag_ssem.at[o], ag_rsem.at[o], dev(b, p)
            ).wait_recv()
        col = jnp.transpose(jnp.broadcast_to(nlw_all[b, :1, :], (128, 128)))[:comp, :1]

        def second(i, carry):
            at = pl.ds(pl.multiple_of(i * rows, rows), rows)
            dots = lax.dot_general(
                gathered[b], unit[at, :], NT, preferred_element_type=jnp.float32
            )
            e = jnp.exp(KAPPA * dots + col)
            part[i] = part[i] + jnp.sum(e.reshape(comp // 8, 8, rows), 0)
            return carry

        lax.fori_loop(0, GROUP, second, 0)

    fin_copies = []
    for m in range(1, GROUP):
        q = plane(m)
        c = remote(part.at[q], part_recv.at[m], fin_ssem.at[m], fin_rsem.at[m], dev(z, q))
        c.start()
        fin_copies.append(c)
    final = part[p]
    for m in range(1, GROUP):
        fin_copies[m - 1].wait_recv()
        final = final + part_recv[m]
    lse_ref[...] = jnp.log(jnp.sum(final, 0, keepdims=True))

    for c in sends + sum_copies + cnt_copies + rs_copies + ag_copies + fin_copies:
        c.wait_send()


def local(n, embeddings, centroids, log_weights):
    rows, depth = embeddings.shape
    total = centroids.shape[0]
    zs = n // GROUP
    comp = total // n
    comps = zs * comp
    dchunk = 256
    chunks = depth // dchunk
    grows = GROUP * rows
    p = lax.axis_index("rows") % GROUP
    own_lw = lax.dynamic_index_in_dim(
        log_weights.reshape(zs, GROUP, comp), p, 1, keepdims=False
    ).reshape(comps, 1)
    dma = pltpu.SemaphoreType.DMA
    vmem = pl.BlockSpec(memory_space=pltpu.VMEM)
    bf16, f32 = jnp.bfloat16, jnp.float32
    direction, nlw, lse = pl.pallas_call(
        functools.partial(kernel, zs, n * rows, dchunk),
        out_shape=(
            jax.ShapeDtypeStruct((comp, depth), bf16),
            jax.ShapeDtypeStruct((1, comp), f32),
            jax.ShapeDtypeStruct((1, rows), f32),
        ),
        in_specs=[vmem, pl.BlockSpec(memory_space=pl.ANY), vmem],
        out_specs=(vmem, vmem, vmem),
        scratch_shapes=[
            pltpu.VMEM((grows, depth), bf16),
            pltpu.VMEM((comps, depth), bf16),
            pltpu.VMEM((comps, grows), f32),
            pltpu.VMEM((comps, grows), bf16),
            pltpu.VMEM((8, grows), f32),
            pltpu.VMEM((GROUP, 8, grows), f32),
            pltpu.VMEM((chunks, zs, comp, dchunk), bf16),
            pltpu.VMEM((chunks, zs, comp, dchunk), bf16),
            pltpu.VMEM((zs, 8, 128), f32),
            pltpu.VMEM((zs, 8, 128), f32),
            pltpu.VMEM((comp, depth), f32),
            pltpu.VMEM((zs, comp, depth), bf16),
            pltpu.VMEM((zs, 8, 128), f32),
            pltpu.VMEM((GROUP, 8, rows), f32),
            pltpu.VMEM((GROUP, 8, rows), f32),
            dma((zs,)),
            dma((GROUP, 2)), dma((GROUP, 2)),
            dma((chunks, zs)), dma((chunks, zs)),
            dma((GROUP,)), dma((GROUP,)),
            dma((zs,)), dma((zs,)),
            dma((zs,)), dma((zs,)),
            dma((zs,)), dma((zs,)),
            dma((GROUP,)), dma((GROUP,)),
        ],
        compiler_params=pltpu.CompilerParams(
            collective_id=0, has_side_effects=True, vmem_limit_bytes=60 * 1024 * 1024
        ),
    )(embeddings, centroids, own_lw)
    return direction, nlw.reshape(comp), lse.reshape(rows)


def solution(mesh):
    return jax.shard_map(
        functools.partial(local, mesh.shape["rows"]),
        mesh=mesh,
        in_specs=(P(("grp", "rows"), None), P(), P()),
        out_specs=(P(("grp", "rows"), None), P(("grp", "rows")), P(("grp", "rows"))),
        check_vma=False,
    )
```

time: 313 us -> 131 us (0.42)
  waiting for transfers between devices: 221 us -> 0 us
  Pallas kernels: 0 us -> 125 us
  blocking collectives: 43.1 us -> 0 us
  matrix products: 26.1 us -> 0 us
  between operations: 14.1 us -> 0.67 us
  other arithmetic: 6.64 us -> 0 us
  local copies, waits for them, and re-layouts: 1.2 us -> 5.68 us
    reduce_scatter x1 -> x0, waiting for transfers between devices: 186 us -> none  [local(): lax.psum_scatter(term_sums, 'rows', scatter_dimension=0, tiled=True)]
    pallas_call x0 -> x1, Pallas kernels: none -> 125 us  [local(): pl.pallas_call(functools.partial(kernel, zs, n * rows, dchunk), out_shape...]
    psum x1 -> x0, blocking collectives: 43.1 us -> none  [local(): counts = lax.psum(jnp.sum(responsible.astype(jnp.float32), 0), 'rows')]
    all_gather x1 -> x0, waiting for transfers between devices: 35.6 us -> none  [local(): lax.all_gather(directions, 'rows', axis=0, tiled=True)]
    dot_general x3 -> x0, matrix products: 26.1 us -> none  [the longest x1 9.04 us: local(): jnp.dot(unit_rows, lax.all_gather(directions, 'rows', axis=0, tiled=True)...]
    unnamed x4 -> x5, local copies, waits for them, and re-layouts: 0.01 us -> 4.82 us
    reduce_sum x3 -> x0, other arithmetic: 4.77 us -> none  [the longest x1 2.11 us: local(): counts = lax.psum(jnp.sum(responsible.astype(jnp.float32), 0), 'rows')]
  transfers between devices with their start and end apart: 2 -> 0, of which waited for: 2 -> 0; matrix products, arithmetic and copies ran while one was open for 0% -> 0% of each run, Pallas kernels for 0% -> 0%
where the time goes in v1:
time: 131 us
  Pallas kernels  125 us (95%)
  local copies, waits for them, and re-layouts  5.68 us (4%)
    pallas_call x1, Pallas kernels, local(): pl.pallas_call(functools.partial(kernel, zs, n * rows, dchunk), out_shape...  125 us
    unnamed x5, local copies, waits for them, and re-layouts  4.82 us

profile of v1, /device:TPU:0, one launch (start us, length us, event | category | flops | bytes accessed | tf_op | source)
XLA Modules:
  0.0 131.1 jit_solution(1377632427332783562)
XLA Ops:
  0.6 0.0 copy-start
  0.7 0.7 copy-done
  1.4 0.9 copy.6.lw_ref
  2.2 124.8 %shard_map.58 = (bf16[128,1024]{1,0:T(8,128)(2,1)}, f32[1,128]{1,0:T(1,128)}, f32[1,512]{1,0:T(1,128)}) custom-call(bf16[512,1024]{1,0:T(8,128)(2,1)} %emb_ref.1, bf16[4096,1024]{1,0:T(8,128)(2,1)} %cent_hbm.1, f32[512,1]{1,0:T(8,128)} %copy.6.lw_ref), custom_call_target="tpu_custom_call" | custom-call | tf_op jit(solution)/shard_map/pallas_call | solution.py:272
  127.0 1.7 %copy.10 = bf16[128,1024]{1,0:T(8,128)(2,1)} copy(bf16[128,1024]{1,0:T(8,128)(2,1)} %get-tuple-element.12) | data formatting | bytes 524288
  128.7 1.2 copy.11
  129.9 1.3 copy.12
  (1 shorter events, 0.0 us)
Async XLA Ops:
  0.6 0.7 copy-start

commit v2 on v1

v2 whole, which is shorter than its diff:
```python
import functools

import jax
import jax.numpy as jnp
from jax import lax
from jax.experimental import pallas as pl
from jax.experimental.pallas import tpu as pltpu
from jax.sharding import PartitionSpec as P

KAPPA = 32
GROUP = 8
MESH = pl.DeviceIdType.MESH
NT = (((1,), (1,)), ((), ()))


def kernel(
    reps, nrows, dchunk, emb_ref, cent_hbm, lw_ref, dir_ref, nlw_ref, lse_ref,
    unit, cent, expo, resp, rsum, rsum_all, y_send, y_recv, z_send, z_recv, cnt_send, cnt_recv,
    own_sum, gathered, nlw_all, part, part_recv,
    cent_sem, row_ssem, row_rsem, y_ssem, y_rsem, z_ssem, z_rsem, sc_ssem, sc_rsem,
    cn_ssem, cn_rsem, ag_ssem, ag_rsem, own_ssem, own_rsem, fwd_ssem, fwd_rsem,
    nl_ssem, nl_rsem, fin_ssem, fin_rsem,
):
    rows, depth = emb_ref.shape
    half = rows // 2
    comp = dir_ref.shape[0]
    chunks = depth // dchunk
    zs = 2 * reps
    me = lax.axis_index("rows")
    p = me % 4 + 4 * ((me // 8) % 2)
    y = (me // 4) % 2
    h = me // 16
    mine = y * reps + h

    def plane(mask):
        q = p
        for bit in (1, 2, 4):
            if mask & bit:
                q = q + bit - 2 * bit * ((p // bit) % 2)
        return q

    def rank(q, yy, hh):
        return q % 4 + 4 * yy + 8 * (q // 4) + 16 * hh

    def dev(q, yy, hh):
        return {"rows": rank(q, yy, hh)}

    def mate(mask):
        return dev(plane(mask), y, h)

    def replica(o):
        b = (mine + o) % zs
        return dev(p, b // reps, b % reps)

    def remote(src, dst, ssem, rsem, to):
        return pltpu.make_async_remote_copy(
            src_ref=src, dst_ref=dst, send_sem=ssem, recv_sem=rsem,
            device_id=to, device_id_type=MESH,
        )

    barrier = pltpu.get_barrier_semaphore()
    for mask in range(1, GROUP):
        pl.semaphore_signal(barrier, inc=1, device_id=mate(mask), device_id_type=MESH)
    for o in range(1, zs):
        pl.semaphore_signal(barrier, inc=1, device_id=replica(o), device_id_type=MESH)

    cent_copies = [
        pltpu.make_async_copy(
            cent_hbm.at[pl.ds(rank(p, b // reps, b % reps) * comp, comp)],
            cent.at[pl.ds(b * comp, comp)],
            cent_sem.at[b],
        )
        for b in range(zs)
    ]
    for c in cent_copies:
        c.start()

    embed = emb_ref[...].astype(jnp.float32)
    unit[pl.ds(p * rows, rows), :] = (
        embed * lax.rsqrt(jnp.sum(embed * embed, 1, keepdims=True) + 1e-06)
    ).astype(jnp.bfloat16)
    pl.semaphore_wait(barrier, GROUP - 1 + zs - 1)

    def row_copy(dst, blk, hf):
        where = unit.at[pl.ds(plane(blk) * rows + hf * half, half)]
        m = blk ^ dst
        return remote(
            where, where, row_ssem.at[m, hf], row_rsem.at[m, hf], mate(dst)
        )

    def arrived(m, hf):
        where = unit.at[pl.ds(plane(m) * rows + hf * half, half)]
        remote(where, where, row_ssem.at[m, hf], row_rsem.at[m, hf], mate(1)).wait_recv()

    sends = []

    def send(dst, blk, hf):
        c = row_copy(dst, blk, hf)
        c.start()
        sends.append(c)

    send(2, 0, 0)
    send(4, 0, 1)
    send(1, 0, 0)
    send(2, 0, 1)
    send(4, 0, 0)
    send(1, 0, 1)
    for c in cent_copies:
        c.wait()

    def score(m, hf):
        base = plane(m) * rows + hf * half
        at = pl.ds(pl.multiple_of(base, half), half)
        dots = lax.dot_general(cent[...], unit[at, :], NT, preferred_element_type=jnp.float32)
        e = jnp.exp(KAPPA * dots + lw_ref[...])
        expo[:, at] = e
        rsum[pl.ds(plane(m) * 2 + hf, 1), :] = jnp.sum(e, 0, keepdims=True)

    score(0, 0)
    score(0, 1)
    arrived(2, 0)
    send(4, 2, 0)
    send(1, 2, 0)
    arrived(4, 1)
    send(2, 4, 1)
    send(1, 4, 1)
    for hf in (0, 1):
        arrived(1, hf)
        score(1, hf)
    score(2, 0)
    score(4, 1)
    arrived(2, 1)
    send(1, 2, 1)
    arrived(4, 0)
    send(1, 4, 0)
    score(2, 1)
    score(4, 0)
    for m, hf in ((3, 0), (5, 1), (3, 1), (5, 0)):
        arrived(m, hf)
        score(m, hf)
    for hf in (0, 1):
        arrived(6, hf)
        send(1, 6, hf)
    for hf in (0, 1):
        score(6, hf)
    for hf in (0, 1):
        arrived(7, hf)
        score(7, hf)

    sum_copies = []
    for m in range(1, GROUP):
        c = remote(rsum, rsum_all.at[m], sc_ssem.at[m], sc_rsem.at[m], mate(m))
        c.start()
        sum_copies.append(c)
    for c in sum_copies:
        c.wait_recv()
    total = rsum[...]
    for m in range(1, GROUP):
        total = total + rsum_all[m]
    rsum_all[0] = 1.0 / total

    def normalise(i, carry):
        at = pl.ds(pl.multiple_of(i * half, half), half)
        inv = rsum_all[0, pl.ds(i, 1), :]
        resp[:, at] = (expo[:, at] * inv).astype(jnp.bfloat16)
        return carry

    lax.fori_loop(0, 2 * GROUP, normalise, 0)

    cnt_copies = []
    ones = jnp.ones((8, GROUP * rows), jnp.bfloat16)
    for b in range(zs):
        cnt_send[b, :, :comp] = lax.dot_general(
            ones, resp[pl.ds(b * comp, comp), :], NT, preferred_element_type=jnp.float32
        )
    for o in range(1, zs):
        to = (mine + o) % zs
        c = remote(cnt_send.at[to], cnt_recv.at[o], cn_ssem.at[o], cn_rsem.at[o], replica(o))
        c.start()
        cnt_copies.append(c)

    side = reps * comp
    y_copies = []
    for d in range(chunks):
        cols = pl.ds(d * dchunk, dchunk)
        expo[:, cols] = jnp.dot(resp[...], unit[:, cols], preferred_element_type=jnp.float32)
        other = pl.ds(pl.multiple_of((1 - y) * side, side), side)
        y_send[d] = expo[other, cols].astype(jnp.bfloat16)
        c = remote(
            y_send.at[d], y_recv.at[d], y_ssem.at[d], y_rsem.at[d], dev(p, 1 - y, h)
        )
        c.start()
        y_copies.append(c)

    for c in cnt_copies:
        c.wait_recv()
    count = cnt_send[mine]
    for o in range(1, zs):
        count = count + cnt_recv[o]
    nlw = jnp.log(count[:, :comp] / nrows)
    nlw_all[mine, :, :comp] = nlw
    nlw_ref[...] = nlw[:1]
    nl_copies = []
    for o in range(1, zs):
        c = remote(
            nlw_all.at[mine], nlw_all.at[mine], nl_ssem.at[o], nl_rsem.at[o], replica(o)
        )
        c.start()
        nl_copies.append(c)

    def both(d, hh):
        cols = pl.ds(d * dchunk, dchunk)
        kept = expo[pl.ds(pl.multiple_of(y * side + hh * comp, comp), comp), cols]
        return kept + y_recv[d, pl.ds(pl.multiple_of(hh * comp, comp), comp), :].astype(jnp.float32)

    z_copies = []
    for d in range(chunks):
        y_copies[d].wait_recv()
        for o in range(1, reps):
            hh = (h + o) % reps
            z_send[d, o] = both(d, hh).astype(jnp.bfloat16)
            c = remote(
                z_send.at[d, o], z_recv.at[d, o], z_ssem.at[d, o], z_rsem.at[d, o], dev(p, y, hh)
            )
            c.start()
            z_copies.append(c)
        own_sum[:, pl.ds(d * dchunk, dchunk)] = both(d, h)

    square = jnp.zeros((comp, 1), jnp.float32)
    for d in range(chunks):
        cols = pl.ds(d * dchunk, dchunk)
        got = own_sum[:, cols]
        for o in range(1, reps):
            z_copies[d * (reps - 1) + o - 1].wait_recv()
            got = got + z_recv[d, o].astype(jnp.float32)
        own_sum[:, cols] = got
        square = square + jnp.sum(got * got, 1, keepdims=True)
    direction = (own_sum[...] * lax.rsqrt(square + 1e-06)).astype(jnp.bfloat16)
    gathered[mine] = direction
    dir_ref[...] = direction

    hc = comp // 2

    def piece(b, hf):
        return gathered.at[b, pl.ds(hf * hc, hc)]

    ag_copies = []
    for hf in range(2):
        for o in range(1, reps):
            where = piece(mine, hf)
            c = remote(
                where, where, ag_ssem.at[o, hf], ag_rsem.at[o, hf], dev(p, y, (h + o) % reps)
            )
            c.start()
            ag_copies.append(c)
    own_copy = remote(
        gathered.at[mine], gathered.at[mine], own_ssem.at[0], own_rsem.at[0], dev(p, 1 - y, h)
    )
    own_copy.start()

    part[...] = jnp.zeros_like(part)

    def second(b):
        col = jnp.transpose(jnp.broadcast_to(nlw_all[b, :1, :], (128, 128)))[:comp, :1]

        def body(i, carry):
            at = pl.ds(pl.multiple_of(i * rows, rows), rows)
            dots = lax.dot_general(
                gathered[b], unit[at, :], NT, preferred_element_type=jnp.float32
            )
            e = jnp.exp(KAPPA * dots + col)
            part[i] = part[i] + jnp.sum(e.reshape(comp // 8, 8, rows), 0)
            return carry

        lax.fori_loop(0, GROUP, body, 0)

    fwd_copies = []

    def forward(hf):
        for o in range(1, reps):
            where = piece(y * reps + (h + reps - o) % reps, hf)
            remote(where, where, ag_ssem.at[o, hf], ag_rsem.at[o, hf], dev(p, y, (h + o) % reps)).wait_recv()
            c = remote(
                where, where, fwd_ssem.at[o, hf], fwd_rsem.at[o, hf], dev(p, 1 - y, h)
            )
            c.start()
            fwd_copies.append(c)

    second(mine)
    for c in nl_copies:
        c.wait_recv()
    forward(0)
    own_copy.wait_recv()
    second((1 - y) * reps + h)
    forward(1)
    for o in range(1, reps):
        second(y * reps + (h + reps - o) % reps)
    for o in range(1, reps):
        b = (1 - y) * reps + (h + reps - o) % reps
        for hf in range(2):
            where = piece(b, hf)
            remote(where, where, fwd_ssem.at[o, hf], fwd_rsem.at[o, hf], dev(p, 1 - y, h)).wait_recv()
        second(b)

    fin_copies = []
    for m in range(1, GROUP):
        q = plane(m)
        c = remote(part.at[q], part_recv.at[m], fin_ssem.at[m], fin_rsem.at[m], mate(m))
        c.start()
        fin_copies.append(c)
    final = part[p]
    for m in range(1, GROUP):
        fin_copies[m - 1].wait_recv()
        final = final + part_recv[m]
    lse_ref[...] = jnp.log(jnp.sum(final, 0, keepdims=True))

    for c in sends + sum_copies + cnt_copies + y_copies + nl_copies + z_copies:
        c.wait_send()
    for c in ag_copies + [own_copy] + fwd_copies + fin_copies:
        c.wait_send()


def local(n, embeddings, centroids, log_weights):
    rows, depth = embeddings.shape
    total = centroids.shape[0]
    zs = n // GROUP
    comp = total // n
    comps = zs * comp
    dchunk = 256
    chunks = depth // dchunk
    grows = GROUP * rows
    reps = zs // 2
    me = lax.axis_index("rows")
    split = log_weights.reshape(reps, 2, 2, 4, comp)
    split = lax.dynamic_slice(
        split, (0, (me // 8) % 2, 0, me % 4, 0), (reps, 1, 2, 1, comp)
    )
    own_lw = split.reshape(reps, 2, comp).swapaxes(0, 1).reshape(comps, 1)
    dma = pltpu.SemaphoreType.DMA
    vmem = pl.BlockSpec(memory_space=pltpu.VMEM)
    bf16, f32 = jnp.bfloat16, jnp.float32
    direction, nlw, lse = pl.pallas_call(
        functools.partial(kernel, reps, n * rows, dchunk),
        out_shape=(
            jax.ShapeDtypeStruct((comp, depth), bf16),
            jax.ShapeDtypeStruct((1, comp), f32),
            jax.ShapeDtypeStruct((1, rows), f32),
        ),
        in_specs=[vmem, pl.BlockSpec(memory_space=pl.ANY), vmem],
        out_specs=(vmem, vmem, vmem),
        scratch_shapes=[
            pltpu.VMEM((grows, depth), bf16),
            pltpu.VMEM((comps, depth), bf16),
            pltpu.VMEM((comps, grows), f32),
            pltpu.VMEM((comps, grows), bf16),
            pltpu.VMEM((2 * GROUP, rows // 2), f32),
            pltpu.VMEM((GROUP, 2 * GROUP, rows // 2), f32),
            pltpu.VMEM((chunks, reps * comp, dchunk), bf16),
            pltpu.VMEM((chunks, reps * comp, dchunk), bf16),
            pltpu.VMEM((chunks, reps, comp, dchunk), bf16),
            pltpu.VMEM((chunks, reps, comp, dchunk), bf16),
            pltpu.VMEM((zs, 8, 128), f32),
            pltpu.VMEM((zs, 8, 128), f32),
            pltpu.VMEM((comp, depth), f32),
            pltpu.VMEM((zs, comp, depth), bf16),
            pltpu.VMEM((zs, 8, 128), f32),
            pltpu.VMEM((GROUP, 8, rows), f32),
            pltpu.VMEM((GROUP, 8, rows), f32),
            dma((zs,)),
            dma((GROUP, 2)), dma((GROUP, 2)),
            dma((chunks,)), dma((chunks,)),
            dma((chunks, reps)), dma((chunks, reps)),
            dma((GROUP,)), dma((GROUP,)),
            dma((zs,)), dma((zs,)),
            dma((reps, 2)), dma((reps, 2)),
            dma((1,)), dma((1,)),
            dma((reps, 2)), dma((reps, 2)),
            dma((zs,)), dma((zs,)),
            dma((GROUP,)), dma((GROUP,)),
        ],
        compiler_params=pltpu.CompilerParams(
            collective_id=0, has_side_effects=True, vmem_limit_bytes=60 * 1024 * 1024
        ),
    )(embeddings, centroids, own_lw)
    return direction, nlw.reshape(comp), lse.reshape(rows)


def solution(mesh):
    return jax.shard_map(
        functools.partial(local, mesh.shape["rows"]),
        mesh=mesh,
        in_specs=(P(("grp", "rows"), None), P(), P()),
        out_specs=(P(("grp", "rows"), None), P(("grp", "rows")), P(("grp", "rows"))),
        check_vma=False,
    )
```

time: 131 us -> 107 us (0.82)
  Pallas kernels: 125 us -> 100 us
    pallas_call x1, Pallas kernels: 125 us -> 100 us  [local(): pl.pallas_call(functools.partial(kernel, reps, n * rows, dchunk), out_sha...]
where the time goes in v2:
time: 107 us
  Pallas kernels  100 us (93%)
  local copies, waits for them, and re-layouts  5.66 us (5%)
    pallas_call x1, Pallas kernels, local(): pl.pallas_call(functools.partial(kernel, reps, n * rows, dchunk), out_sha...  100 us
    unnamed x5, local copies, waits for them, and re-layouts  4.79 us

profile of v2, /device:TPU:0, one launch (start us, length us, event | category | flops | bytes accessed | tf_op | source)
XLA Modules:
  0.0 106.7 jit_solution(9953126304179024284)
XLA Ops:
  0.6 0.0 copy-start
  0.7 0.7 copy-done
  1.4 0.9 copy.8.lw_ref
  2.2 100.4 %shard_map.58 = (bf16[128,1024]{1,0:T(8,128)(2,1)}, f32[1,128]{1,0:T(1,128)}, f32[1,512]{1,0:T(1,128)}) custom-call(bf16[512,1024]{1,0:T(8,128)(2,1)} %emb_ref.1, bf16[4096,1024]{1,0:T(8,128)(2,1)} %cent_hbm.1, f32[512,1]{1,0:T(8,128)} %copy.8.lw_ref), custom_call_target="tpu_custom_call" | custom-call | tf_op jit(solution)/shard_map/pallas_call | solution.py:342
  102.6 1.7 %copy.12 = bf16[128,1024]{1,0:T(8,128)(2,1)} copy(bf16[128,1024]{1,0:T(8,128)(2,1)} %get-tuple-element.12) | data formatting | bytes 524288
  104.3 1.2 %copy.13 = f32[128]{0:T(128)} copy(f32[128]{0:T(128)} %bitcast.11) | data formatting | bytes 1024
  105.5 1.3 %copy.14 = f32[512]{0:T(512)} copy(f32[512]{0:T(512)} %bitcast.10) | data formatting | bytes 4096
  (2 shorter events, 0.0 us)
Async XLA Ops:
  0.6 0.7 copy-start

commit v3 on v2

--- a/solution.py
+++ b/solution.py
@@ -16,7 +16,7 @@
 def kernel(
     reps, nrows, dchunk, emb_ref, cent_hbm, lw_ref, dir_ref, nlw_ref, lse_ref,
     unit, cent, expo, resp, rsum, rsum_all, y_send, y_recv, z_send, z_recv, cnt_send, cnt_recv,
-    own_sum, gathered, nlw_all, part, part_recv,
+    own_sum, gathered, nlw_all, part, part_recv, lw_row, lw_col,
     cent_sem, row_ssem, row_rsem, y_ssem, y_rsem, z_ssem, z_rsem, sc_ssem, sc_rsem,
     cn_ssem, cn_rsem, ag_ssem, ag_rsem, own_ssem, own_rsem, fwd_ssem, fwd_rsem,
     nl_ssem, nl_rsem, fin_ssem, fin_rsem,
@@ -26,6 +26,7 @@
     comp = dir_ref.shape[0]
     chunks = depth // dchunk
     zs = 2 * reps
+    hc = comp // 2
     me = lax.axis_index("rows")
     p = me % 4 + 4 * ((me // 8) % 2)
     y = (me // 4) % 2
@@ -66,14 +67,24 @@
 
     cent_copies = [
         pltpu.make_async_copy(
-            cent_hbm.at[pl.ds(rank(p, b // reps, b % reps) * comp, comp)],
-            cent.at[pl.ds(b * comp, comp)],
-            cent_sem.at[b],
+            cent_hbm.at[pl.ds(rank(p, b // reps, b % reps) * comp + c * hc, hc)],
+            cent.at[pl.ds((c * zs + b) * hc, hc)],
+            cent_sem.at[c, b],
         )
+        for c in range(2)
         for b in range(zs)
     ]
     for c in cent_copies:
         c.start()
+
+    def column(row):
+        return jnp.transpose(jnp.broadcast_to(row, (128, 128)))[:comp, :1]
+
+    for b in range(zs):
+        lw_row[:1, :comp] = lw_ref[pl.ds(rank(p, b // reps, b % reps), 1), :]
+        col = column(lw_row[:1, :])
+        for c in range(2):
+            lw_col[pl.ds((c * zs + b) * hc, hc), :] = col[c * hc : (c + 1) * hc]
 
     embed = emb_ref[...].astype(jnp.float32)
     unit[pl.ds(p * rows, rows), :] = (
@@ -112,7 +123,7 @@
         base = plane(m) * rows + hf * half
         at = pl.ds(pl.multiple_of(base, half), half)
         dots = lax.dot_general(cent[...], unit[at, :], NT, preferred_element_type=jnp.float32)
-        e = jnp.exp(KAPPA * dots + lw_ref[...])
+        e = jnp.exp(KAPPA * dots + lw_col[...])
         expo[:, at] = e
         rsum[pl.ds(plane(m) * 2 + hf, 1), :] = jnp.sum(e, 0, keepdims=True)
 
@@ -167,31 +178,89 @@
 
     lax.fori_loop(0, 2 * GROUP, normalise, 0)
 
+    side = reps * hc
+    y_copies = {}
+    for c in range(2):
+        for d in range(chunks):
+            cols = pl.ds(d * dchunk, dchunk)
+            expo[pl.ds(c * zs * hc, zs * hc), cols] = jnp.dot(
+                resp[pl.ds(c * zs * hc, zs * hc), :], unit[:, cols],
+                preferred_element_type=jnp.float32,
+            )
+            other = pl.ds(pl.multiple_of(c * zs * hc + (1 - y) * side, side), side)
+            y_send[c, d] = expo[other, cols].astype(jnp.bfloat16)
+            y_copies[c, d] = remote(
+                y_send.at[c, d], y_recv.at[c, d], y_ssem.at[c, d], y_rsem.at[c, d],
+                dev(p, 1 - y, h),
+            )
+            y_copies[c, d].start()
+
     cnt_copies = []
     ones = jnp.ones((8, GROUP * rows), jnp.bfloat16)
     for b in range(zs):
-        cnt_send[b, :, :comp] = lax.dot_general(
-            ones, resp[pl.ds(b * comp, comp), :], NT, preferred_element_type=jnp.float32
-        )
+        for c in range(2):
+            cnt_send[b, :, c * hc : (c + 1) * hc] = lax.dot_general(
+                ones, resp[pl.ds((c * zs + b) * hc, hc), :], NT,
+                preferred_element_type=jnp.float32,
+            )
     for o in range(1, zs):
         to = (mine + o) % zs
         c = remote(cnt_send.at[to], cnt_recv.at[o], cn_ssem.at[o], cn_rsem.at[o], replica(o))
         c.start()
         cnt_copies.append(c)
 
-    side = reps * comp
-    y_copies = []
-    for d in range(chunks):
+    def both(c, d, hh):
         cols = pl.ds(d * dchunk, dchunk)
-        expo[:, cols] = jnp.dot(resp[...], unit[:, cols], preferred_element_type=jnp.float32)
-        other = pl.ds(pl.multiple_of((1 - y) * side, side), side)
-        y_send[d] = expo[other, cols].astype(jnp.bfloat16)
-        c = remote(
-            y_send.at[d], y_recv.at[d], y_ssem.at[d], y_rsem.at[d], dev(p, 1 - y, h)
-        )
-        c.start()
-        y_copies.append(c)
-
+        kept = expo[pl.ds(pl.multiple_of(c * zs * hc + y * side + hh * hc, hc), hc), cols]
+        return kept + y_recv[c, d, pl.ds(pl.multiple_of(hh * hc, hc), hc), :].astype(jnp.float32)
+
+    z_copies = {}
+
+    def over_z(c):
+        for d in range(chunks):
+            y_copies[c, d].wait_recv()
+            for o in range(1, reps):
+                hh = (h + o) % reps
+                z_send[c, d, o] = both(c, d, hh).astype(jnp.bfloat16)
+                z_copies[c, d, o] = remote(
+                    z_send.at[c, d, o], z_recv.at[c, d, o], z_ssem.at[c, d, o],
+                    z_rsem.at[c, d, o], dev(p, y, hh),
+                )
+                z_copies[c, d, o].start()
+            own_sum[pl.ds(c * hc, hc), pl.ds(d * dchunk, dchunk)] = both(c, d, h)
+
+    def piece(b, c):
+        return gathered.at[b, pl.ds(c * hc, hc)]
+
+    ag_copies = []
+    own_copies = []
+
+    def finish(c):
+        here = pl.ds(c * hc, hc)
+        square = jnp.zeros((hc, 1), jnp.float32)
+        for d in range(chunks):
+            cols = pl.ds(d * dchunk, dchunk)
+            got = own_sum[here, cols]
+            for o in range(1, reps):
+                z_copies[c, d, o].wait_recv()
+                got = got + z_recv[c, d, o].astype(jnp.float32)
+            own_sum[here, cols] = got
+            square = square + jnp.sum(got * got, 1, keepdims=True)
+        direction = (own_sum[here, :] * lax.rsqrt(square + 1e-06)).astype(jnp.bfloat16)
+        gathered[mine, here, :] = direction
+        dir_ref[here, :] = direction
+        where = piece(mine, c)
+        for o in range(1, reps):
+            copy = remote(
+                where, where, ag_ssem.at[o, c], ag_rsem.at[o, c], dev(p, y, (h + o) % reps)
+            )
+            copy.start()
+            ag_copies.append(copy)
+        copy = remote(where, where, own_ssem.at[c], own_rsem.at[c], dev(p, 1 - y, h))
+        copy.start()
+        own_copies.append(copy)
+
+    over_z(0)
     for c in cnt_copies:
         c.wait_recv()
     count = cnt_send[mine]
@@ -207,61 +276,14 @@
         )
         c.start()
         nl_copies.append(c)
-
-    def both(d, hh):
-        cols = pl.ds(d * dchunk, dchunk)
-        kept = expo[pl.ds(pl.multiple_of(y * side + hh * comp, comp), comp), cols]
-        return kept + y_recv[d, pl.ds(pl.multiple_of(hh * comp, comp), comp), :].astype(jnp.float32)
-
-    z_copies = []
-    for d in range(chunks):
-        y_copies[d].wait_recv()
-        for o in range(1, reps):
-            hh = (h + o) % reps
-            z_send[d, o] = both(d, hh).astype(jnp.bfloat16)
-            c = remote(
-                z_send.at[d, o], z_recv.at[d, o], z_ssem.at[d, o], z_rsem.at[d, o], dev(p, y, hh)
-            )
-            c.start()
-            z_copies.append(c)
-        own_sum[:, pl.ds(d * dchunk, dchunk)] = both(d, h)
-
-    square = jnp.zeros((comp, 1), jnp.float32)
-    for d in range(chunks):
-        cols = pl.ds(d * dchunk, dchunk)
-        got = own_sum[:, cols]
-        for o in range(1, reps):
-            z_copies[d * (reps - 1) + o - 1].wait_recv()
-            got = got + z_recv[d, o].astype(jnp.float32)
-        own_sum[:, cols] = got
-        square = square + jnp.sum(got * got, 1, keepdims=True)
-    direction = (own_sum[...] * lax.rsqrt(square + 1e-06)).astype(jnp.bfloat16)
-    gathered[mine] = direction
-    dir_ref[...] = direction
-
-    hc = comp // 2
-
-    def piece(b, hf):
-        return gathered.at[b, pl.ds(hf * hc, hc)]
-
-    ag_copies = []
-    for hf in range(2):
-        for o in range(1, reps):
-            where = piece(mine, hf)
-            c = remote(
-                where, where, ag_ssem.at[o, hf], ag_rsem.at[o, hf], dev(p, y, (h + o) % reps)
-            )
-            c.start()
-            ag_copies.append(c)
-    own_copy = remote(
-        gathered.at[mine], gathered.at[mine], own_ssem.at[0], own_rsem.at[0], dev(p, 1 - y, h)
-    )
-    own_copy.start()
+    finish(0)
+    over_z(1)
+    finish(1)
 
     part[...] = jnp.zeros_like(part)
 
     def second(b):
-        col = jnp.transpose(jnp.broadcast_to(nlw_all[b, :1, :], (128, 128)))[:comp, :1]
+        col = column(nlw_all[b, :1, :])
 
         def body(i, carry):
             at = pl.ds(pl.multiple_of(i * rows, rows), rows)
@@ -286,11 +308,10 @@
             c.start()
             fwd_copies.append(c)
 
+    forward(0)
     second(mine)
-    for c in nl_copies:
+    for c in nl_copies + own_copies:
         c.wait_recv()
-    forward(0)
-    own_copy.wait_recv()
     second((1 - y) * reps + h)
     forward(1)
     for o in range(1, reps):
@@ -312,12 +333,20 @@
     for m in range(1, GROUP):
         fin_copies[m - 1].wait_recv()
         final = final + part_recv[m]
-    lse_ref[...] = jnp.log(jnp.sum(final, 0, keepdims=True))
-
-    for c in sends + sum_copies + cnt_copies + y_copies + nl_copies + z_copies:
+    lse_ref[...] = jnp.sum(final, 0, keepdims=True)
+
+    for c in sends + sum_copies + cnt_copies + nl_copies:
         c.wait_send()
-    for c in ag_copies + [own_copy] + fwd_copies + fin_copies:
+    for c in list(y_copies.values()) + list(z_copies.values()):
         c.wait_send()
+    for c in ag_copies + own_copies + fwd_copies + fin_copies:
+        c.wait_send()
+
+
+def settle(direction, nlw, lse, direction_out, nlw_out, lse_out):
+    direction_out[...] = direction[...]
+    nlw_out[...] = nlw[...]
+    lse_out[...] = jnp.log(lse[...])
 
 
 def local(n, embeddings, centroids, log_weights):
@@ -330,12 +359,7 @@
     chunks = depth // dchunk
     grows = GROUP * rows
     reps = zs // 2
-    me = lax.axis_index("rows")
-    split = log_weights.reshape(reps, 2, 2, 4, comp)
-    split = lax.dynamic_slice(
-        split, (0, (me // 8) % 2, 0, me % 4, 0), (reps, 1, 2, 1, comp)
-    )
-    own_lw = split.reshape(reps, 2, comp).swapaxes(0, 1).reshape(comps, 1)
+    hc = comp // 2
     dma = pltpu.SemaphoreType.DMA
     vmem = pl.BlockSpec(memory_space=pltpu.VMEM)
     bf16, f32 = jnp.bfloat16, jnp.float32
@@ -355,10 +379,10 @@
             pltpu.VMEM((comps, grows), bf16),
             pltpu.VMEM((2 * GROUP, rows // 2), f32),
             pltpu.VMEM((GROUP, 2 * GROUP, rows // 2), f32),
-            pltpu.VMEM((chunks, reps * comp, dchunk), bf16),
-            pltpu.VMEM((chunks, reps * comp, dchunk), bf16),
-            pltpu.VMEM((chunks, reps, comp, dchunk), bf16),
-            pltpu.VMEM((chunks, reps, comp, dchunk), bf16),
+            pltpu.VMEM((2, chunks, reps * hc, dchunk), bf16),
+            pltpu.VMEM((2, chunks, reps * hc, dchunk), bf16),
+            pltpu.VMEM((2, chunks, reps, hc, dchunk), bf16),
+            pltpu.VMEM((2, chunks, reps, hc, dchunk), bf16),
             pltpu.VMEM((zs, 8, 128), f32),
             pltpu.VMEM((zs, 8, 128), f32),
             pltpu.VMEM((comp, depth), f32),
@@ -366,14 +390,16 @@
             pltpu.VMEM((zs, 8, 128), f32),
             pltpu.VMEM((GROUP, 8, rows), f32),
             pltpu.VMEM((GROUP, 8, rows), f32),
-            dma((zs,)),
+            pltpu.VMEM((8, 128), f32),
+            pltpu.VMEM((comps, 1), f32),
+            dma((2, zs)),
             dma((GROUP, 2)), dma((GROUP, 2)),
-            dma((chunks,)), dma((chunks,)),
-            dma((chunks, reps)), dma((chunks, reps)),
+            dma((2, chunks)), dma((2, chunks)),
+            dma((2, chunks, reps)), dma((2, chunks, reps)),
             dma((GROUP,)), dma((GROUP,)),
             dma((zs,)), dma((zs,)),
             dma((reps, 2)), dma((reps, 2)),
-            dma((1,)), dma((1,)),
+            dma((2,)), dma((2,)),
             dma((reps, 2)), dma((reps, 2)),
             dma((zs,)), dma((zs,)),
             dma((GROUP,)), dma((GROUP,)),
@@ -381,7 +407,17 @@
         compiler_params=pltpu.CompilerParams(
             collective_id=0, has_side_effects=True, vmem_limit_bytes=60 * 1024 * 1024
         ),
-    )(embeddings, centroids, own_lw)
+    )(embeddings, centroids, log_weights.reshape(n, comp))
+    direction, nlw, lse = pl.pallas_call(
+        settle,
+        out_shape=(
+            jax.ShapeDtypeStruct((comp, depth), bf16),
+            jax.ShapeDtypeStruct((1, comp), f32),
+            jax.ShapeDtypeStruct((1, rows), f32),
+        ),
+        in_specs=[vmem, vmem, vmem],
+        out_specs=(vmem, vmem, vmem),
+    )(direction, nlw, lse)
     return direction, nlw.reshape(comp), lse.reshape(rows)
 
 

time: 107 us -> 106 us (level)
  Pallas kernels: 100 us -> 106 us
  local copies, waits for them, and re-layouts: 5.66 us -> 0 us
    unnamed x5 -> x0, local copies, waits for them, and re-layouts: 4.79 us -> none
    pallas_call x1, Pallas kernels: 100 us -> 104 us  [local(): pl.pallas_call(functools.partial(kernel, reps, n * rows, dchunk), out_sha...]
    pallas_call x0 -> x1, Pallas kernels: none -> 1.68 us  [local(): pl.pallas_call(settle, out_shape=(jax.ShapeDtypeStruct((comp, depth), bf1...]
where the time goes in v3:
time: 106 us
  Pallas kernels  106 us (100%)
    pallas_call x1, Pallas kernels, local(): pl.pallas_call(functools.partial(kernel, reps, n * rows, dchunk), out_sha...  104 us

profile of v3, /device:TPU:0, one launch (start us, length us, event | category | flops | bytes accessed | tf_op | source)
XLA Modules:
  0.0 106.2 jit_solution(2793008865505728717)
XLA Ops:
  0.6 103.8 %shard_map.58 = (bf16[128,1024]{1,0:T(8,128)(2,1)}, f32[1,128]{1,0:T(1,128)}, f32[1,512]{1,0:T(1,128)}) custom-call(bf16[512,1024]{1,0:T(8,128)(2,1)} %emb_ref.1, bf16[4096,1024]{1,0:T(8,128)(2,1)} %cent_hbm.1, f32[32,128]{1,0:T(8,128)} %bitcast.3), custom_call_target="tpu_custom_call" | custom-call | tf_op jit(solution)/shard_map/pallas_call | solution.py:366
  104.5 1.7 %shard_map.59 = (bf16[128,1024]{1,0:T(8,128)(2,1)}, f32[1,128]{1,0:T(1,128)}, f32[1,512]{1,0:T(1,128)}) custom-call(bf16[128,1024]{1,0:T(8,128)(2,1)} %get-tuple-element.9.direction, f32[1,128]{1,0:T(1,128)} %get-tuple-element.10.nlw, f32[1,512]{1,0:T(1,128)} %get-tuple-element.11.lse), custom_call_target="tpu_custom_call" | custom-call | tf_op jit(solution)/shard_map/pallas_call | solution.py:411

commit v4 on v3

--- a/solution.py
+++ b/solution.py
@@ -80,16 +80,14 @@
     def column(row):
         return jnp.transpose(jnp.broadcast_to(row, (128, 128)))[:comp, :1]
 
-    for b in range(zs):
-        lw_row[:1, :comp] = lw_ref[pl.ds(rank(p, b // reps, b % reps), 1), :]
-        col = column(lw_row[:1, :])
-        for c in range(2):
-            lw_col[pl.ds((c * zs + b) * hc, hc), :] = col[c * hc : (c + 1) * hc]
-
-    embed = emb_ref[...].astype(jnp.float32)
-    unit[pl.ds(p * rows, rows), :] = (
-        embed * lax.rsqrt(jnp.sum(embed * embed, 1, keepdims=True) + 1e-06)
-    ).astype(jnp.bfloat16)
+    def unit_half(hf):
+        here = pl.ds(hf * half, half)
+        embed = emb_ref[here, :].astype(jnp.float32)
+        unit[pl.ds(pl.multiple_of(p * rows + hf * half, half), half), :] = (
+            embed * lax.rsqrt(jnp.sum(embed * embed, 1, keepdims=True) + 1e-06)
+        ).astype(jnp.bfloat16)
+
+    unit_half(0)
     pl.semaphore_wait(barrier, GROUP - 1 + zs - 1)
 
     def row_copy(dst, blk, hf):
@@ -110,12 +108,17 @@
         c.start()
         sends.append(c)
 
-    send(2, 0, 0)
-    send(4, 0, 1)
-    send(1, 0, 0)
-    send(2, 0, 1)
-    send(4, 0, 0)
-    send(1, 0, 1)
+    for hf in (0, 1):
+        if hf:
+            unit_half(hf)
+        send(2, 0, hf)
+        send(4, 0, hf)
+        send(1, 0, hf)
+    for b in range(zs):
+        lw_row[:1, :comp] = lw_ref[pl.ds(rank(p, b // reps, b % reps), 1), :]
+        col = column(lw_row[:1, :])
+        for c in range(2):
+            lw_col[pl.ds((c * zs + b) * hc, hc), :] = col[c * hc : (c + 1) * hc]
     for c in cent_copies:
         c.wait()
 
@@ -180,6 +183,25 @@
 
     side = reps * hc
     y_copies = {}
+    def both(c, d, hh):
+        cols = pl.ds(d * dchunk, dchunk)
+        kept = expo[pl.ds(pl.multiple_of(c * zs * hc + y * side + hh * hc, hc), hc), cols]
+        return kept + y_recv[c, d, pl.ds(pl.multiple_of(hh * hc, hc), hc), :].astype(jnp.float32)
+
+    z_copies = {}
+
+    def over_z(c, d):
+        y_copies[c, d].wait_recv()
+        for o in range(1, reps):
+            hh = (h + o) % reps
+            z_send[c, d, o] = both(c, d, hh).astype(jnp.bfloat16)
+            z_copies[c, d, o] = remote(
+                z_send.at[c, d, o], z_recv.at[c, d, o], z_ssem.at[c, d, o],
+                z_rsem.at[c, d, o], dev(p, y, hh),
+            )
+            z_copies[c, d, o].start()
+        own_sum[pl.ds(c * hc, hc), pl.ds(d * dchunk, dchunk)] = both(c, d, h)
+
     for c in range(2):
         for d in range(chunks):
             cols = pl.ds(d * dchunk, dchunk)
@@ -194,6 +216,8 @@
                 dev(p, 1 - y, h),
             )
             y_copies[c, d].start()
+            if c:
+                over_z(0, d)
 
     cnt_copies = []
     ones = jnp.ones((8, GROUP * rows), jnp.bfloat16)
@@ -208,26 +232,6 @@
         c = remote(cnt_send.at[to], cnt_recv.at[o], cn_ssem.at[o], cn_rsem.at[o], replica(o))
         c.start()
         cnt_copies.append(c)
-
-    def both(c, d, hh):
-        cols = pl.ds(d * dchunk, dchunk)
-        kept = expo[pl.ds(pl.multiple_of(c * zs * hc + y * side + hh * hc, hc), hc), cols]
-        return kept + y_recv[c, d, pl.ds(pl.multiple_of(hh * hc, hc), hc), :].astype(jnp.float32)
-
-    z_copies = {}
-
-    def over_z(c):
-        for d in range(chunks):
-            y_copies[c, d].wait_recv()
-            for o in range(1, reps):
-                hh = (h + o) % reps
-                z_send[c, d, o] = both(c, d, hh).astype(jnp.bfloat16)
-                z_copies[c, d, o] = remote(
-                    z_send.at[c, d, o], z_recv.at[c, d, o], z_ssem.at[c, d, o],
-                    z_rsem.at[c, d, o], dev(p, y, hh),
-                )
-                z_copies[c, d, o].start()
-            own_sum[pl.ds(c * hc, hc), pl.ds(d * dchunk, dchunk)] = both(c, d, h)
 
     def piece(b, c):
         return gathered.at[b, pl.ds(c * hc, hc)]
@@ -260,7 +264,9 @@
         copy.start()
         own_copies.append(copy)
 
-    over_z(0)
+    finish(0)
+    for d in range(chunks):
+        over_z(1, d)
     for c in cnt_copies:
         c.wait_recv()
     count = cnt_send[mine]
@@ -276,8 +282,6 @@
         )
         c.start()
         nl_copies.append(c)
-    finish(0)
-    over_z(1)
     finish(1)
 
     part[...] = jnp.zeros_like(part)

time: 106 us -> 102 us (0.962)
  Pallas kernels: 106 us -> 101 us
    pallas_call x1, Pallas kernels: 104 us -> 99.4 us  [local(): pl.pallas_call(functools.partial(kernel, reps, n * rows, dchunk), out_sha...]
where the time goes in v4:
time: 102 us
  Pallas kernels  101 us (99%)
    pallas_call x1, Pallas kernels, local(): pl.pallas_call(functools.partial(kernel, reps, n * rows, dchunk), out_sha...  99.4 us

profile of v4, /device:TPU:0, one launch (start us, length us, event | category | flops | bytes accessed | tf_op | source)
XLA Modules:
  0.0 101.7 jit_solution(7810751444357581234)
XLA Ops:
  0.6 99.4 %shard_map.58 = (bf16[128,1024]{1,0:T(8,128)(2,1)}, f32[1,128]{1,0:T(1,128)}, f32[1,512]{1,0:T(1,128)}) custom-call(bf16[512,1024]{1,0:T(8,128)(2,1)} %emb_ref.1, bf16[4096,1024]{1,0:T(8,128)(2,1)} %cent_hbm.1, f32[32,128]{1,0:T(8,128)} %bitcast.3), custom_call_target="tpu_custom_call" | custom-call | tf_op jit(solution)/shard_map/pallas_call | solution.py:370
  100.0 1.7 %shard_map.59 = (bf16[128,1024]{1,0:T(8,128)(2,1)}, f32[1,128]{1,0:T(1,128)}, f32[1,512]{1,0:T(1,128)}) custom-call(bf16[128,1024]{1,0:T(8,128)(2,1)} %get-tuple-element.9.direction, f32[1,128]{1,0:T(1,128)} %get-tuple-element.10.nlw, f32[1,512]{1,0:T(1,128)} %get-tuple-element.11.lse), custom_call_target="tpu_custom_call" | custom-call | tf_op jit(solution)/shard_map/pallas_call | solution.py:415

commit v5 on v4

--- a/solution.py
+++ b/solution.py
@@ -219,20 +219,6 @@
             if c:
                 over_z(0, d)
 
-    cnt_copies = []
-    ones = jnp.ones((8, GROUP * rows), jnp.bfloat16)
-    for b in range(zs):
-        for c in range(2):
-            cnt_send[b, :, c * hc : (c + 1) * hc] = lax.dot_general(
-                ones, resp[pl.ds((c * zs + b) * hc, hc), :], NT,
-                preferred_element_type=jnp.float32,
-            )
-    for o in range(1, zs):
-        to = (mine + o) % zs
-        c = remote(cnt_send.at[to], cnt_recv.at[o], cn_ssem.at[o], cn_rsem.at[o], replica(o))
-        c.start()
-        cnt_copies.append(c)
-
     def piece(b, c):
         return gathered.at[b, pl.ds(c * hc, hc)]
 
@@ -265,8 +251,22 @@
         own_copies.append(copy)
 
     finish(0)
+    cnt_copies = []
+    ones = jnp.ones((8, GROUP * rows), jnp.bfloat16)
+    for b in range(zs):
+        for c in range(2):
+            cnt_send[b, :, c * hc : (c + 1) * hc] = lax.dot_general(
+                ones, resp[pl.ds((c * zs + b) * hc, hc), :], NT,
+                preferred_element_type=jnp.float32,
+            )
+    for o in range(1, zs):
+        to = (mine + o) % zs
+        c = remote(cnt_send.at[to], cnt_recv.at[o], cn_ssem.at[o], cn_rsem.at[o], replica(o))
+        c.start()
+        cnt_copies.append(c)
     for d in range(chunks):
         over_z(1, d)
+    finish(1)
     for c in cnt_copies:
         c.wait_recv()
     count = cnt_send[mine]
@@ -282,7 +282,6 @@
         )
         c.start()
         nl_copies.append(c)
-    finish(1)
 
     part[...] = jnp.zeros_like(part)
 

time: 102 us -> 104 us (1.020)
  Pallas kernels: 101 us -> 104 us
    pallas_call x1, Pallas kernels: 99.4 us -> 102 us  [local(): pl.pallas_call(functools.partial(kernel, reps, n * rows, dchunk), out_sha...]
where the time goes in v5:
time: 104 us
  Pallas kernels  104 us (100%)
    pallas_call x1, Pallas kernels, local(): pl.pallas_call(functools.partial(kernel, reps, n * rows, dchunk), out_sha...  102 us

profile of v5, /device:TPU:0, one launch (start us, length us, event | category | flops | bytes accessed | tf_op | source)
XLA Modules:
  0.0 104.2 jit_solution(6158437660100763783)
XLA Ops:
  0.6 101.8 %shard_map.58 = (bf16[128,1024]{1,0:T(8,128)(2,1)}, f32[1,128]{1,0:T(1,128)}, f32[1,512]{1,0:T(1,128)}) custom-call(bf16[512,1024]{1,0:T(8,128)(2,1)} %emb_ref.1, bf16[4096,1024]{1,0:T(8,128)(2,1)} %cent_hbm.1, f32[32,128]{1,0:T(8,128)} %bitcast.3), custom_call_target="tpu_custom_call" | custom-call | tf_op jit(solution)/shard_map/pallas_call | solution.py:369
  102.5 1.7 %shard_map.59 = (bf16[128,1024]{1,0:T(8,128)(2,1)}, f32[1,128]{1,0:T(1,128)}, f32[1,512]{1,0:T(1,128)}) custom-call(bf16[128,1024]{1,0:T(8,128)(2,1)} %get-tuple-element.9.direction, f32[1,128]{1,0:T(1,128)} %get-tuple-element.10.nlw, f32[1,512]{1,0:T(1,128)} %get-tuple-element.11.lse), custom_call_target="tpu_custom_call" | custom-call | tf_op jit(solution)/shard_map/pallas_call | solution.py:414
